TPU v7x, 256 devices: a whole 4x4x8 slice. The times are simulated.
256 devices in a mesh: tm: 16 (over x_hi, z), inner: 16 (over y, x_lo, core).
Axes of the slice: x: 4 (x_hi: 2, x_lo: 2; x = x_hi * 2 + x_lo), y: 4, z: 8, core: 2. Of those that a mesh axis runs over, the one named last changes fastest.
Arguments:
- start_panels: float32 [16, 192, 2048], P('tm', None, 'inner'), may hold values from -6 to 6
- kinetic: float32 [2048, 2048], P('inner')
- fields: int32 [16, 2048], P('tm'), may hold values from -1 to 1, as said below
Outputs:
- orbitals: float32 [16, 8, 192, 2048], P('tm', None, None, 'inner')
- log_scales: float32 [16, 8, 192], P('tm')
Inputs may be any that keep to these rules, and one draw needn't show every extreme that they name: `fields`: each entry is -1 or +1.
All inputs are finite; a program needn't handle non-finite values.
Results may differ from a plain program's by a relative error of at most 0.0003.
Values sent between devices are 32-bit elements; how exact they have to be, the bound alone decides.
No kernel may reach another device: no remote copies, remote signals or barrier semaphores. Data moves between devices by JAX's collectives and lax.ppermute only.
A program may use at most 128 MiB of HBM per device.

v0:
```python
import math

import jax
import jax.numpy as jnp
from jax import lax
from jax.sharding import PartitionSpec as P

coupling = 0.17725


def from_behind(block, axis, distance):
    devices = range(lax.axis_size(axis))
    route = [((i - distance) % len(devices), i) for i in devices]
    return lax.ppermute(block, axis, route)


def contract_last(left, right):
    return lax.dot_general(
        left,
        right,
        (((1,), (1,)), ((), ())),
        precision=lax.Precision.HIGHEST,
        preferred_element_type=jnp.float32,
    )


def factor_panel(panel, gram_matrix):
    lower = jnp.linalg.cholesky(gram_matrix)
    orthonormal = lax.linalg.triangular_solve(lower, panel, left_side=True, lower=True)
    return (orthonormal, jnp.log(jnp.diagonal(lower)))


def on_device(start_panels, kinetic, fields):
    rows = kinetic.shape[0]
    sites = kinetic.shape[1]
    rank = lax.axis_index("inner")
    hops = lax.axis_size("tm") // 2
    first = rank * rows
    scales = jnp.exp(coupling * fields.astype(jnp.float32))
    orbit_list = []
    log_list = []
    own_scales = lax.dynamic_slice_in_dim(scales, first, rows, 1)
    own_block = start_panels[0]
    for hop in range(hops):
        own_block = (
            contract_last(lax.all_gather(own_block, "inner", axis=1, tiled=True), kinetic)
            * own_scales[0][None, :]
        )
        gram_matrix = lax.psum(contract_last(own_block, own_block), "inner")
        own_block, log_diag = factor_panel(own_block, gram_matrix)
        orbit_list.append(math.sqrt(sites) * own_block)
        log_list.append(log_diag)
        if hop + 1 < hops:
            own_block = from_behind(own_block, "tm", 1)
    return (jnp.stack(orbit_list, 0)[None], jnp.stack(log_list, 0)[None])


def solution(mesh):
    placed = (P("tm", None, "inner"), P("inner", None), P("tm", None))
    return jax.shard_map(
        on_device,
        mesh=mesh,
        in_specs=placed,
        out_specs=(P("tm", None, None, "inner"), P("tm", None, None)),
        check_vma=False,
    )
```

profile of v0, /device:TPU:1, one launch (start us, length us, event | category | flops | bytes accessed | tf_op | source)
XLA Modules:
  0.0 1765.3 jit_solution(9818129227126943744)
XLA Ops:
  8.6 43.4 %all-gather.24.cloned.1.call-done = f32[1,192,2048]{2,1,0:T(8,128)} async-done(((f32[1,192,128]{2,1,0:T(8,128)}), f32[1,192,2048]{2,1,0:T(8,128)}) %all-gather.24.cloned.1.call-update) | async-done | bytes 1572880 | tf_op jit(solution)/shard_map/all_gather | solution.py:46
  56.0 115.6 %all-reduce.12.cloned.1.call-done = f32[192,192]{0,1:T(8,128)} async-done(((f32[192,192]{0,1:T(8,128)}), f32[192,192]{0,1:T(8,128)}) %all-reduce.12.cloned.1.call-update) | async-done | bytes 147472 | tf_op jit(solution)/shard_map/psum | solution.py:49
  173.6 11.7 cholesky.412
  185.9 9.8 custom-call.41
  204.1 19.7 %custom-call.42 = f32[2,128,128]{1,2,0:T(8,128)S(1)} custom-call(f32[2,128,128]{2,1,0:T(8,128)S(1)} %pad_maximum_fusion), custom_call_target="InvertDiagBlocksLowerTriangular" | custom-call | tf_op jit(solution)/shard_map/triangular_solve/custom-call.0 | solution.py:29
  225.7 6.2 collective-permute-done
  232.8 36.1 %all-gather.10.cloned.1.call-done = f32[192,2048]{1,0:T(8,128)} async-done(((f32[192,128]{1,0:T(8,128)}), f32[192,2048]{1,0:T(8,128)}) %all-gather.10.cloned.1.call-update) | async-done | bytes 1572880 | tf_op jit(solution)/shard_map/all_gather | solution.py:46
  272.8 115.6 %all-reduce.14.cloned.1.call-done = f32[192,192]{0,1:T(8,128)} async-done(((f32[192,192]{0,1:T(8,128)}), f32[192,192]{0,1:T(8,128)}) %all-reduce.14.cloned.1.call-update) | async-done | bytes 147472 | tf_op jit(solution)/shard_map/psum | solution.py:49
  390.5 11.7 cholesky.450
  402.9 9.8 custom-call.43
  421.0 19.7 %custom-call.44 = f32[2,128,128]{1,2,0:T(8,128)S(1)} custom-call(f32[2,128,128]{2,1,0:T(8,128)S(1)} %pad_maximum_fusion.1), custom_call_target="InvertDiagBlocksLowerTriangular" | custom-call | tf_op jit(solution)/shard_map/triangular_solve/custom-call.0 | solution.py:29
  441.5 10.5 collective-permute-start.1
  452.0 6.2 collective-permute-done.1
  458.9 36.4 %all-gather.12.cloned.1.call-done = f32[192,2048]{1,0:T(8,128)} async-done(((f32[192,128]{1,0:T(8,128)}), f32[192,2048]{1,0:T(8,128)}) %all-gather.12.cloned.1.call-update) | async-done | bytes 1572880 | tf_op jit(solution)/shard_map/all_gather | solution.py:46
  499.2 115.4 %all-reduce.16.cloned.1.call-done = f32[192,192]{0,1:T(8,128)} async-done(((f32[192,192]{0,1:T(8,128)}), f32[192,192]{0,1:T(8,128)}) %all-reduce.16.cloned.1.call-update) | async-done | bytes 147472 | tf_op jit(solution)/shard_map/psum | solution.py:49
  616.6 11.7 cholesky.488
  629.0 9.8 custom-call.45
  647.2 19.7 %custom-call.46 = f32[2,128,128]{1,2,0:T(8,128)S(1)} custom-call(f32[2,128,128]{2,1,0:T(8,128)S(1)} %pad_maximum_fusion.2), custom_call_target="InvertDiagBlocksLowerTriangular" | custom-call | tf_op jit(solution)/shard_map/triangular_solve/custom-call.0 | solution.py:29
  668.7 6.2 collective-permute-done.2
  676.0 36.0 %all-gather.14.cloned.1.call-done = f32[192,2048]{1,0:T(8,128)} async-done(((f32[192,128]{1,0:T(8,128)}), f32[192,2048]{1,0:T(8,128)}) %all-gather.14.cloned.1.call-update) | async-done | bytes 1572880 | tf_op jit(solution)/shard_map/all_gather | solution.py:46
  715.9 115.6 %all-reduce.18.cloned.1.call-done = f32[192,192]{0,1:T(8,128)} async-done(((f32[192,192]{0,1:T(8,128)}), f32[192,192]{0,1:T(8,128)}) %all-reduce.18.cloned.1.call-update) | async-done | bytes 147472 | tf_op jit(solution)/shard_map/psum | solution.py:49
  833.5 11.7 cholesky.526
  845.9 9.8 custom-call.47
  864.1 19.7 %custom-call.48 = f32[2,128,128]{1,2,0:T(8,128)S(1)} custom-call(f32[2,128,128]{2,1,0:T(8,128)S(1)} %pad_maximum_fusion.3), custom_call_target="InvertDiagBlocksLowerTriangular" | custom-call | tf_op jit(solution)/shard_map/triangular_solve/custom-call.0 | solution.py:29
  885.8 6.2 collective-permute-done.3
  892.7 36.4 %all-gather.16.cloned.1.call-done = f32[192,2048]{1,0:T(8,128)} async-done(((f32[192,128]{1,0:T(8,128)}), f32[192,2048]{1,0:T(8,128)}) %all-gather.16.cloned.1.call-update) | async-done | bytes 1572880 | tf_op jit(solution)/shard_map/all_gather | solution.py:46
  932.9 115.4 %all-reduce.20.cloned.1.call-done = f32[192,192]{0,1:T(8,128)} async-done(((f32[192,192]{0,1:T(8,128)}), f32[192,192]{0,1:T(8,128)}) %all-reduce.20.cloned.1.call-update) | async-done | bytes 147472 | tf_op jit(solution)/shard_map/psum | solution.py:49
  1050.4 11.7 cholesky.564
  1062.8 9.8 custom-call.49
  1081.0 19.7 %custom-call.50 = f32[2,128,128]{1,2,0:T(8,128)S(1)} custom-call(f32[2,128,128]{2,1,0:T(8,128)S(1)} %pad_maximum_fusion.4), custom_call_target="InvertDiagBlocksLowerTriangular" | custom-call | tf_op jit(solution)/shard_map/triangular_solve/custom-call.0 | solution.py:29
  1102.5 6.2 collective-permute-done.4
  1109.8 36.0 %all-gather.18.cloned.1.call-done = f32[192,2048]{1,0:T(8,128)} async-done(((f32[192,128]{1,0:T(8,128)}), f32[192,2048]{1,0:T(8,128)}) %all-gather.18.cloned.1.call-update) | async-done | bytes 1572880 | tf_op jit(solution)/shard_map/all_gather | solution.py:46
  1149.7 115.6 %all-reduce.22.cloned.1.call-done = f32[192,192]{0,1:T(8,128)} async-done(((f32[192,192]{0,1:T(8,128)}), f32[192,192]{0,1:T(8,128)}) %all-reduce.22.cloned.1.call-update) | async-done | bytes 147472 | tf_op jit(solution)/shard_map/psum | solution.py:49
  1267.3 11.7 cholesky.602
  1279.7 9.8 custom-call.51
  1297.9 19.7 %custom-call.52 = f32[2,128,128]{1,2,0:T(8,128)S(1)} custom-call(f32[2,128,128]{2,1,0:T(8,128)S(1)} %pad_maximum_fusion.5), custom_call_target="InvertDiagBlocksLowerTriangular" | custom-call | tf_op jit(solution)/shard_map/triangular_solve/custom-call.0 | solution.py:29
  1319.6 6.2 collective-permute-done.5
  1326.5 36.4 %all-gather.20.cloned.1.call-done = f32[192,2048]{1,0:T(8,128)} async-done(((f32[192,128]{1,0:T(8,128)}), f32[192,2048]{1,0:T(8,128)}) %all-gather.20.cloned.1.call-update) | async-done | bytes 1572880 | tf_op jit(solution)/shard_map/all_gather | solution.py:46
  1366.7 115.6 %all-reduce.24.cloned.1.call-done = f32[192,192]{0,1:T(8,128)} async-done(((f32[192,192]{0,1:T(8,128)}), f32[192,192]{0,1:T(8,128)}) %all-reduce.24.cloned.1.call-update) | async-done | bytes 147472 | tf_op jit(solution)/shard_map/psum | solution.py:49
  1484.3 11.7 cholesky.640
  1496.8 9.8 custom-call.53
  1515.6 20.5 %custom-call.54 = f32[2,128,128]{1,2,0:T(8,128)S(1)} custom-call(f32[2,128,128]{2,1,0:T(8,128)} %pad_maximum_fusion.6), custom_call_target="InvertDiagBlocksLowerTriangular" | custom-call | tf_op jit(solution)/shard_map/triangular_solve/custom-call.0 | solution.py:29
  1539.3 6.2 collective-permute-done.6
  1559.3 23.3 %all-gather.22.cloned.1.call-done = f32[192,2048]{1,0:T(8,128)} async-done(((f32[192,128]{1,0:T(8,128)}), f32[192,2048]{1,0:T(8,128)}) %all-gather.22.cloned.1.call-update) | async-done | bytes 1572880 | tf_op jit(solution)/shard_map/all_gather | solution.py:46
  1591.6 110.5 %all-reduce.26.cloned.1.call-done = f32[192,192]{0,1:T(8,128)} async-done(((f32[192,192]{0,1:T(8,128)}), f32[192,192]{0,1:T(8,128)}) %all-reduce.26.cloned.1.call-update) | async-done | bytes 147472 | tf_op jit(solution)/shard_map/psum | solution.py:49
  1704.1 11.7 cholesky.678
  1716.5 9.8 custom-call.55
  1736.7 19.7 %custom-call.56 = f32[2,128,128]{1,2,0:T(8,128)S(1)} custom-call(f32[2,128,128]{2,1,0:T(8,128)S(1)} %pad_maximum_fusion.7), custom_call_target="InvertDiagBlocksLowerTriangular" | custom-call | tf_op jit(solution)/shard_map/triangular_solve/custom-call.0 | solution.py:29
  (263 shorter events, 152.0 us)
Async XLA Ops:
  7.2 44.9 %copy-start = (f32[128,2048]{1,0:T(8,128)S(1)}, f32[128,2048]{1,0:T(8,128)}, u32[]{:S(2)}) copy-start(f32[128,2048]{1,0:T(8,128)} %param.7) | copy-start | bytes 3145732
  7.2 44.9 %all-gather.24.cloned.1.call-start = ((), (), s32[]{:S(2)}) async-start(), calls=%async_computation.15 | async-start | bytes 1671168 | tf_op jit(solution)/shard_map/all_gather | solution.py:46
  7.9 163.6 %all-reduce.12.cloned.1.call-start = ((), (), s32[]{:S(2)}) async-start(), calls=%async_computation | async-start | bytes 393216 | tf_op jit(solution)/shard_map/psum | solution.py:49
  55.9 213.1 %all-gather.10.cloned.1.call-start = ((), (), s32[]{:S(2)}) async-start(), calls=%async_computation.1 | async-start | bytes 1671168 | tf_op jit(solution)/shard_map/all_gather | solution.py:46
  224.6 7.3 collective-permute-start
  231.8 0.6 copy-start.4
  232.5 155.9 %all-reduce.14.cloned.1.call-start = ((), (), s32[]{:S(2)}) async-start(), calls=%async_computation.2 | async-start | bytes 393216 | tf_op jit(solution)/shard_map/psum | solution.py:49
  272.8 222.5 %all-gather.12.cloned.1.call-start = ((), (), s32[]{:S(2)}) async-start(), calls=%async_computation.3 | async-start | bytes 1671168 | tf_op jit(solution)/shard_map/all_gather | solution.py:46
  441.5 16.7 collective-permute-start.1
  458.2 0.6 copy-start.5
  458.8 155.7 %all-reduce.16.cloned.1.call-start = ((), (), s32[]{:S(2)}) async-start(), calls=%async_computation.4 | async-start | bytes 393216 | tf_op jit(solution)/shard_map/psum | solution.py:49
  499.1 212.9 %all-gather.14.cloned.1.call-start = ((), (), s32[]{:S(2)}) async-start(), calls=%async_computation.5 | async-start | bytes 1671168 | tf_op jit(solution)/shard_map/all_gather | solution.py:46
  667.6 7.3 collective-permute-start.2
  674.9 0.6 copy-start.6
  675.6 155.9 %all-reduce.18.cloned.1.call-start = ((), (), s32[]{:S(2)}) async-start(), calls=%async_computation.6 | async-start | bytes 393216 | tf_op jit(solution)/shard_map/psum | solution.py:49
  715.8 213.2 %all-gather.16.cloned.1.call-start = ((), (), s32[]{:S(2)}) async-start(), calls=%async_computation.7 | async-start | bytes 1671168 | tf_op jit(solution)/shard_map/all_gather | solution.py:46
  884.5 7.4 collective-permute-start.3
  892.0 0.6 copy-start.7
  892.6 155.7 %all-reduce.20.cloned.1.call-start = ((), (), s32[]{:S(2)}) async-start(), calls=%async_computation.8 | async-start | bytes 393216 | tf_op jit(solution)/shard_map/psum | solution.py:49
  932.9 212.9 %all-gather.18.cloned.1.call-start = ((), (), s32[]{:S(2)}) async-start(), calls=%async_computation.9 | async-start | bytes 1671168 | tf_op jit(solution)/shard_map/all_gather | solution.py:46
  1101.4 7.3 collective-permute-start.4
  1108.7 0.6 copy-start.8
  1109.3 155.9 %all-reduce.22.cloned.1.call-start = ((), (), s32[]{:S(2)}) async-start(), calls=%async_computation.10 | async-start | bytes 393216 | tf_op jit(solution)/shard_map/psum | solution.py:49
  1149.6 213.2 %all-gather.20.cloned.1.call-start = ((), (), s32[]{:S(2)}) async-start(), calls=%async_computation.11 | async-start | bytes 1671168 | tf_op jit(solution)/shard_map/all_gather | solution.py:46
  1318.3 48.4 %copy-start.1 = (f32[64,128]{1,0:T(8,128)}, f32[64,128]{1,0:T(8,128)S(1)}, u32[]{:S(2)}) copy-start(f32[64,128]{1,0:T(8,128)S(1)} %fusion.74) | copy-start | bytes 98308
  1318.3 7.4 collective-permute-start.5
  1325.7 0.6 copy-start.9
  1326.4 155.9 %all-reduce.24.cloned.1.call-start = ((), (), s32[]{:S(2)}) async-start(), calls=%async_computation.12 | async-start | bytes 393216 | tf_op jit(solution)/shard_map/psum | solution.py:49
  1366.7 215.9 %all-gather.22.cloned.1.call-start = ((), (), s32[]{:S(2)}) async-start(), calls=%async_computation.13 | async-start | bytes 1671168 | tf_op jit(solution)/shard_map/all_gather | solution.py:46
  1536.1 0.7 copy-start.10
  1538.2 7.3 collective-permute-start.6
  1545.5 0.6 copy-start.3
  1546.2 155.9 %all-reduce.26.cloned.1.call-start = ((), (), s32[]{:S(2)}) async-start(), calls=%async_computation.14 | async-start | bytes 393216 | tf_op jit(solution)/shard_map/psum | solution.py:49
  1559.3 27.1 %copy-start.2 = (f32[64,128]{1,0:T(8,128)S(1)}, f32[64,128]{1,0:T(8,128)}, u32[]{:S(2)}) copy-start(f32[64,128]{1,0:T(8,128)} %copy-done.1) | copy-start | bytes 98308
Sparse Core Ops, SparseCore 0:
  9.8 42.2 all-gather.23
  56.0 115.4 all-reduce.11
  232.6 36.2 all-gather.9
  272.9 115.4 all-reduce.13
  459.0 36.2 all-gather.11
  499.2 115.3 all-reduce.15
  675.7 36.2 all-gather.13
  716.0 115.4 all-reduce.17
  892.7 36.2 all-gather.15
  933.0 115.3 all-reduce.19
  1109.5 36.2 all-gather.17
  1149.7 115.4 all-reduce.21
  1326.5 36.2 all-gather.19
  1366.8 115.4 all-reduce.23
  1546.3 36.2 all-gather.21
  1586.6 115.4 all-reduce.25
where the time goes:
time: 1780 us; the launch traced here: 1770 us
  waiting for transfers between devices  1250 us (70%)
  other arithmetic  403 us (23%)
  matrix products  39.9 us (2%)
  local copies, waits for them, and re-layouts  29.6 us (2%)
  between operations  26.1 us (1%)
  starting transfers between devices  19.3 us (1%)
    psum x8, waiting for transfers between devices, on_device(): gram_matrix = lax.psum(contract_last(own_block, own_block), 'inner')  919 us
    all_gather x8, waiting for transfers between devices, on_device(): lax.all_gather(own_block, 'inner', axis=1, tiled=True)  284 us
    another operation x56, other arithmetic, factor_panel(): lower = jnp.linalg.cholesky(gram_matrix)  230 us
    another operation x41, other arithmetic, factor_panel(): lax.linalg.triangular_solve(lower, panel, left_side=True, lower=True)  160 us
    ppermute x7, waiting for transfers between devices, from_behind(): return lax.ppermute(block, axis, route)  43.3 us
  transfers between devices with their start and end apart: 23, of which 23 were waited for; matrix products, arithmetic and copies ran while one was open for 1% of the time, Pallas kernels for 0%

commit v1 on v0

v1 whole, which is shorter than its diff:
```python
import math

import jax
import jax.numpy as jnp
from jax import lax
from jax.experimental import pallas as pl
from jax.experimental.pallas import tpu as pltpu
from jax.sharding import PartitionSpec as P

coupling = 0.17725
F32 = jnp.float32
BF16 = jnp.bfloat16
LANES = 128
PIVOTS = 8
BLOCK = 64
CHUNK = 256


def from_behind(block, axis, distance):
    devices = range(lax.axis_size(axis))
    route = [((i - distance) % len(devices), i) for i in devices]
    return lax.ppermute(block, axis, route)


def halves(value):
    high = value.astype(BF16)
    return high, (value - high.astype(F32)).astype(BF16)


def last_with_last(left, right):
    return lax.dot_general(left, right, (((1,), (1,)), ((), ())), preferred_element_type=F32)


def last_with_first(left, right):
    return lax.dot_general(left, right, (((1,), (0,)), ((), ())), preferred_element_type=F32)


def factor(gram_ref, inverse_ref, pivot_ref, beside):
    size = gram_ref.shape[0]
    lane = lax.broadcasted_iota(jnp.int32, (size, LANES), 1)
    row = lax.broadcasted_iota(jnp.int32, (size, LANES), 0)
    sublane = lax.broadcasted_iota(jnp.int32, (PIVOTS, LANES), 0)
    cut = size - LANES
    second = jnp.where(row - LANES == lane - cut, 1.0, 0.0)
    tiles = [
        gram_ref[:, :LANES],
        jnp.where(lane < cut, gram_ref[:, LANES:], second),
        jnp.where(row == lane, 1.0, 0.0),
    ]
    step = 0
    for first in range(0, size, BLOCK):
        last = first + BLOCK
        live = [t for t in range(3) if t > 0 or first < LANES]
        part = {t: tiles[t][:BLOCK] for t in live}
        done = {t: [] for t in live}
        for top in range(0, BLOCK, PIVOTS):
            column = first + top
            source = part[column // LANES]
            height = BLOCK - top
            start = column % LANES
            columns = [
                jnp.broadcast_to(source[:, start + j : start + j + 1], (height, LANES))
                for j in range(PIVOTS)
            ]
            pivots = jnp.zeros((PIVOTS, LANES), F32)
            for j in range(PIVOTS):
                pivots = jnp.where(sublane == j, columns[j][:PIVOTS], pivots)
                scaled = columns[j] * (1.0 / columns[j][j : j + 1, :])
                below = jnp.where(sublane > j, scaled[:PIVOTS], 0.0)
                if height > PIVOTS:
                    below = jnp.concatenate([below, scaled[PIVOTS:]], 0)
                for k in range(j + 1, PIVOTS):
                    columns[k] = columns[k] - below * columns[k][j : j + 1, :]
                for t in live:
                    part[t] = part[t] - below * part[t][j : j + 1, :]
            root = lax.rsqrt(pivots)
            root = root * (1.5 - 0.5 * pivots * root * root)
            pivot_ref[column : column + PIVOTS, :] = pivots
            for t in live:
                done[t].append(part[t][:PIVOTS] * root)
                part[t] = part[t][PIVOTS:]
            beside(step)
            step += 1
        full = {t: jnp.concatenate(done[t], 0) for t in live}
        inverse_ref[first:last, :LANES] = full[2]
        padding = jnp.zeros((BLOCK, LANES - cut), F32)
        corner = full[1][:, cut:] if first >= LANES else jnp.zeros((BLOCK, cut), F32)
        inverse_ref[first:last, LANES:] = jnp.concatenate([corner, padding], 1)
        if last == size:
            break
        if last < LANES:
            left = jnp.concatenate([full[0][:, last:], full[1][:, :cut]], 1)
        else:
            left = full[1][:, last - LANES : cut]
        live = [t for t in range(3) if t > 0 or last < LANES]
        update = lax.dot_general(
            left,
            jnp.concatenate([full[t] for t in live], 1),
            (((0,), (0,)), ((), ())),
            precision=lax.Precision.HIGHEST,
            preferred_element_type=F32,
        )
        for i, t in enumerate(live):
            tiles[t] = tiles[t][BLOCK:] - update[:, LANES * i : LANES * i + LANES]
        if last >= LANES:
            tiles[0] = None


def chain_kernel(
    own_ref,
    panel_ref,
    scale_ref,
    kinetic_ref,
    out_ref,
    kinetic_high,
    kinetic_low,
    buffers,
    arrived,
    panel,
    mapped,
    inverse_pair,
    gram_ref,
    inverse_ref,
    pivot_ref,
):
    rank, sites = panel_ref.shape
    hops = scale_ref.shape[0]
    chunks = sites // CHUNK
    own = pl.multiple_of(own_ref[0] * LANES, LANES)

    def load(c):
        return pltpu.make_async_copy(
            kinetic_ref.at[pl.ds(c * CHUNK, CHUNK), :], buffers.at[c % 2], arrived.at[c % 2]
        )

    def map_chunk(source, hop, c):
        at = slice(c * CHUNK, (c + 1) * CHUNK)
        both = last_with_last(source[...], kinetic_high[at, :])
        rest = last_with_last(source[:rank, :], kinetic_low[at, :])
        return (both[:rank] + both[rank:] + rest) * scale_ref[pl.ds(hop, 1), at]

    def put(target, c, value):
        high, low = halves(value)
        target[:rank, c * CHUNK : (c + 1) * CHUNK] = high
        target[rank:, c * CHUNK : (c + 1) * CHUNK] = low

    load(0).start()
    load(1).start()
    for c in range(chunks):
        put(mapped, c, panel_ref[:, c * CHUNK : (c + 1) * CHUNK])
    for c in range(chunks):
        load(c).wait()
        high, low = halves(buffers[c % 2])
        kinetic_high[c * CHUNK : (c + 1) * CHUNK, :] = high
        kinetic_low[c * CHUNK : (c + 1) * CHUNK, :] = low
        if c + 2 < chunks:
            load(c + 2).start()
        put(panel, c, map_chunk(mapped, 0, c))

    row = lax.broadcasted_iota(jnp.int32, (LANES, LANES), 0)
    lane = lax.broadcasted_iota(jnp.int32, (LANES, LANES), 1)
    diagonal = row == lane
    steps = rank // PIVOTS

    def hop_body(hop, beside):
        both = panel[...]
        products = last_with_last(both, both)
        gram = (products[:rank, :rank] + products[rank:, rank:]) + (
            products[:rank, rank:] + products[rank:, :rank]
        )
        gram_ref[:, :LANES] = gram[:, :LANES]
        gram_ref[:, LANES:] = jnp.concatenate(
            [gram[:, LANES:], jnp.zeros((rank, 2 * LANES - rank), F32)], 1
        )
        factor(gram_ref, inverse_ref, pivot_ref, beside)
        high, low = halves(inverse_ref[:, :rank])
        inverse_pair[:rank, :] = high
        inverse_pair[rank:, :] = low
        mine = panel[:, pl.ds(own, LANES)]
        products = last_with_first(inverse_pair[...], mine[:rank])
        rest = last_with_first(inverse_pair[:rank, :], mine[rank:])
        out_ref[hop, :rank, :] = (products[:rank] + products[rank:] + rest) * math.sqrt(sites)
        upper = jnp.sum(jnp.where(diagonal, pivot_ref[:LANES], 0.0), 0, keepdims=True)
        under = jnp.where(diagonal[: rank - LANES], pivot_ref[LANES:], 0.0)
        under = jnp.sum(under, 0, keepdims=True)
        under = jnp.where(lane[:1] < rank - LANES, under, 1.0)
        out_ref[hop, rank:, :] = jnp.concatenate(
            [0.5 * jnp.log(upper), 0.5 * jnp.log(under), jnp.zeros((6, LANES), F32)], 0
        )

    def whole_hop(hop, carry):
        def beside(step):
            if step % 2 == 1 and step // 2 < chunks:
                put(mapped, step // 2, map_chunk(panel, hop + 1, step // 2))

        hop_body(hop, beside)
        for c in range(chunks):
            at = slice(c * CHUNK, (c + 1) * CHUNK)
            products = last_with_first(inverse_pair[...], mapped[:rank, at])
            rest = last_with_first(inverse_pair[:rank, :], mapped[rank:, at])
            put(panel, c, products[:rank] + products[rank:] + rest)
        return carry

    lax.fori_loop(0, hops - 1, whole_hop, 0)
    hop_body(hops - 1, lambda step: None)


def run_chain(own, panel, scales, kinetic):
    rank, sites = panel.shape
    hops = scales.shape[0]
    return pl.pallas_call(
        chain_kernel,
        out_shape=jax.ShapeDtypeStruct((hops, rank + 8, LANES), F32),
        in_specs=[
            pl.BlockSpec(memory_space=pltpu.SMEM),
            pl.BlockSpec(memory_space=pltpu.VMEM),
            pl.BlockSpec(memory_space=pltpu.VMEM),
            pl.BlockSpec(memory_space=pl.ANY),
        ],
        out_specs=pl.BlockSpec(memory_space=pltpu.VMEM),
        scratch_shapes=[
            pltpu.VMEM((sites, sites), BF16),
            pltpu.VMEM((sites, sites), BF16),
            pltpu.VMEM((2, CHUNK, sites), F32),
            pltpu.SemaphoreType.DMA((2,)),
            pltpu.VMEM((2 * rank, sites), BF16),
            pltpu.VMEM((2 * rank, sites), BF16),
            pltpu.VMEM((2 * rank, rank), BF16),
            pltpu.VMEM((rank, 2 * LANES), F32),
            pltpu.VMEM((rank, 2 * LANES), F32),
            pltpu.VMEM((rank, LANES), F32),
        ],
        compiler_params=pltpu.CompilerParams(vmem_limit_bytes=48 << 20),
        name="chain",
    )(own, panel, scales, kinetic)


def on_device(start_panels, kinetic, fields):
    rank = start_panels.shape[1]
    hops = lax.axis_size("tm") // 2
    away = hops - 1
    scales = jnp.exp(coupling * fields.astype(F32))
    distance = 1
    while distance < hops:
        scales = jnp.concatenate([from_behind(scales, "tm", distance), scales], 0)
        distance *= 2
    panel = from_behind(start_panels[0], "tm", away)
    panel = lax.all_gather(panel, "inner", axis=1, tiled=True)
    whole = lax.all_gather(kinetic, "inner", axis=0, tiled=True)
    own = lax.axis_index("inner").astype(jnp.int32)[None]
    blocks = run_chain(own, panel, scales, whole)
    parts = [from_behind(blocks[k], "tm", k - away) if k < away else blocks[k] for k in range(hops)]
    orbitals = jnp.stack([part[:rank] for part in parts], 0)[None]
    logs = jnp.stack([part[rank : rank + 2].reshape(-1)[:rank] for part in parts], 0)[None]
    return (orbitals, logs)


def solution(mesh):
    placed = (P("tm", None, "inner"), P("inner", None), P("tm", None))
    return jax.shard_map(
        on_device,
        mesh=mesh,
        in_specs=placed,
        out_specs=(P("tm", None, None, "inner"), P("tm", None, None)),
        check_vma=False,
    )
```

time: 1780 us -> 293 us (0.16)
  waiting for transfers between devices: 1250 us -> 149 us
  other arithmetic: 403 us -> 0.8 us
  Pallas kernels: 0 us -> 91.6 us
  matrix products: 39.9 us -> 0 us
  local copies, waits for them, and re-layouts: 29.6 us -> 2.99 us
    psum x8 -> x0, waiting for transfers between devices: 919 us -> none  [on_device(): gram_matrix = lax.psum(contract_last(own_block, own_block), 'inner')]
    another operation x98 -> x0, other arithmetic: 390 us -> none  [the longest x56 230 us: factor_panel(): lower = jnp.linalg.cholesky(gram_matrix)]
    all_gather x8 -> x2, waiting for transfers between devices: 284 us -> 113 us  [the longest x1 96.2 us: on_device(): whole = lax.all_gather(kinetic, 'inner', axis=0, tiled=True)]
    pallas_call x0 -> x1, Pallas kernels: none -> 91.6 us  [run_chain(): pl.pallas_call(chain_kernel, out_shape=jax.ShapeDtypeStruct((hops, rank +...]
    dot_general x16 -> x0, matrix products: 30.6 us -> none  [contract_last(): lax.dot_general(left, right, (((1,), (1,)), ((), ())), precision=lax.Prec...]
    ppermute x7 -> x11, waiting for transfers between devices: 43.3 us -> 35.6 us  [from_behind(): return lax.ppermute(block, axis, route)]
  transfers between devices with their start and end apart: 23 -> 13, of which waited for: 23 -> 8; matrix products, arithmetic and copies ran while one was open for 1% -> 0% of each run, Pallas kernels for 0% -> 0%
where the time goes in v1:
time: 293 us; the launch traced here: 289 us
  waiting for transfers between devices  149 us (51%)
  Pallas kernels  91.6 us (31%)
  starting transfers between devices  30.1 us (10%)
  between operations  14.2 us (5%)
  local copies, waits for them, and re-layouts  2.99 us (1%)
    all_gather x1, waiting for transfers between devices, on_device(): whole = lax.all_gather(kinetic, 'inner', axis=0, tiled=True)  96.2 us
    pallas_call x1, Pallas kernels, run_chain(): pl.pallas_call(chain_kernel, out_shape=jax.ShapeDtypeStruct((hops, rank +...  91.6 us
    ppermute x11, waiting for transfers between devices, from_behind(): return lax.ppermute(block, axis, route)  35.6 us
    ppermute x11, starting transfers between devices, from_behind(): return lax.ppermute(block, axis, route)  30 us
    all_gather x1, waiting for transfers between devices, on_device(): panel = lax.all_gather(panel, 'inner', axis=1, tiled=True)  16.8 us
  transfers between devices with their start and end apart: 13, of which 8 were waited for; matrix products, arithmetic and copies ran while one was open for 0% of the time, Pallas kernels for 0%

profile of v1, /device:TPU:1, one launch (start us, length us, event | category | flops | bytes accessed | tf_op | source)
XLA Modules:
  0.0 289.1 jit_solution(15800051766967334641)
XLA Ops:
  7.2 0.0 all-gather.3.cloned.1.call-start
  7.2 6.5 %collective-permute-start = (f32[192,128]{1,0:T(8,128)}, f32[192,128]{1,0:T(8,128)S(1)}, u32[]{:S(2)}, u32[]{:S(2)}) collective-permute-start(f32[192,128]{1,0:T(8,128)} %bitcast.88), channel_id=1, source_target_pairs={{144,0},{160,16},{176,32},{192,48},{208,64},{224,80},{240,96},{0,1... | collective-permute-start | bytes 294920 | tf_op jit(solution)/shard_map/ppermute | solution.py:22
  13.7 2.0 collective-permute-done
  15.6 0.0 copy-start.1
  15.6 0.6 copy-done.1
  16.3 0.0 all-gather.3.cloned.1.call-update
  16.3 0.0 all-gather.5.cloned.1.call-start
  16.4 0.7 all-gather.5.cloned.1.call-update
  17.1 0.7 multiply_exponential_fusion
  17.8 1.0 collective-permute-start.1
  18.7 5.6 %collective-permute-done.1 = f32[1,2048]{1,0:T(1,128)S(1)} collective-permute-done((f32[1,2048]{1,0:T(1,128)S(1)}, f32[1,2048]{1,0:T(1,128)S(1)}, u32[]{:S(2)}, u32[]{:S(2)}) %collective-permute-start.1) | collective-permute-done | bytes 8224 | tf_op jit(solution)/shard_map/ppermute | solution.py:22
  24.3 0.1 collective-permute-start.2
  24.4 7.1 %collective-permute-done.2 = f32[2,2048]{1,0:T(2,128)S(1)} collective-permute-done((f32[2,2048]{1,0:T(2,128)S(1)}, f32[2,2048]{1,0:T(2,128)S(1)}, u32[]{:S(2)}, u32[]{:S(2)}) %collective-permute-start.2) | collective-permute-done | bytes 16416 | tf_op jit(solution)/shard_map/ppermute | solution.py:22
  31.5 0.6 collective-permute-start.3
  32.1 8.7 %collective-permute-done.3 = f32[4,2048]{1,0:T(4,128)S(1)} collective-permute-done((f32[4,2048]{1,0:T(4,128)S(1)}, f32[4,2048]{1,0:T(4,128)S(1)}, u32[]{:S(2)}, u32[]{:S(2)}) %collective-permute-start.3) | collective-permute-done | bytes 32800 | tf_op jit(solution)/shard_map/ppermute | solution.py:22
  40.9 16.8 %all-gather.3.cloned.1.call-done.panel_ref = f32[192,2048]{1,0:T(8,128)} async-done(((f32[192,128]{1,0:T(8,128)}), f32[192,2048]{1,0:T(8,128)}) %all-gather.3.cloned.1.call-update) | async-done | bytes 1572880 | tf_op jit(solution)/shard_map/all_gather | solution.py:248
  57.7 96.2 %all-gather.5.cloned.1.call-done.kinetic_ref = f32[2048,2048]{1,0:T(8,128)} async-done(((f32[128,2048]{1,0:T(8,128)}), f32[2048,2048]{1,0:T(8,128)}) %all-gather.5.cloned.1.call-update) | async-done | bytes 16777232 | tf_op jit(solution)/shard_map/all_gather | solution.py:249
  154.0 0.0 copy-start
  154.0 1.4 copy-done
  155.4 91.6 %chain.1 = f32[8,200,128]{2,1,0:T(8,128)S(1)} custom-call(s32[1]{0:T(128)} %bitcast.own_ref, f32[192,2048]{1,0:T(8,128)S(1)} %copy-done, f32[8,2048]{1,0:T(8,128)S(1)} %pad_maximum_fusion.scale_ref, f32[2048,2048]{1,0:T(8,128)} %all-gather.5.cloned.1.call-done.kinetic_ref), custom_call_target="tpu_custom_call" | custom-call | tf_op jit(solution)/shard_map/chain/pallas_call | solution.py:211
  247.0 0.1 slice_bitcast_fusion
  247.0 3.8 %collective-permute-start.4 = (f32[200,128]{1,0:T(8,128)S(1)}, f32[200,128]{1,0:T(8,128)S(1)}, u32[]{:S(2)}, u32[]{:S(2)}) collective-permute-start(f32[200,128]{1,0:T(8,128)S(1)} %get-tuple-element.8), channel_id=1, source_target_pairs={{112,0},{128,16},{144,32},{160,48},{176,64},{192,80},{208,96},{224... | collective-permute-start | bytes 307208 | tf_op jit(solution)/shard_map/ppermute | solution.py:22
  250.8 1.9 collective-permute-start.10
  252.7 2.2 collective-permute-start.9
  254.9 2.8 collective-permute-start.8
  257.7 4.1 %collective-permute-start.7 = (f32[200,128]{1,0:T(8,128)S(1)}, f32[200,128]{1,0:T(8,128)S(1)}, u32[]{:S(2)}, u32[]{:S(2)}) collective-permute-start(f32[200,128]{1,0:T(8,128)S(1)} %get-tuple-element.5), channel_id=1, source_target_pairs={{64,0},{80,16},{96,32},{112,48},{128,64},{144,80},{160,96},{176,11... | collective-permute-start | bytes 307208 | tf_op jit(solution)/shard_map/ppermute | solution.py:22
  261.8 0.0 collective-permute-done.4
  261.8 0.7 collective-permute-start.5
  262.5 7.6 %collective-permute-done.5 = f32[200,128]{1,0:T(8,128)S(1)} collective-permute-done((f32[200,128]{1,0:T(8,128)S(1)}, f32[200,128]{1,0:T(8,128)S(1)}, u32[]{:S(2)}, u32[]{:S(2)}) %collective-permute-start.5) | collective-permute-done | bytes 102432 | tf_op jit(solution)/shard_map/ppermute | solution.py:22
  270.1 6.4 %collective-permute-start.6 = (f32[200,128]{1,0:T(8,128)S(1)}, f32[200,128]{1,0:T(8,128)S(1)}, u32[]{:S(2)}, u32[]{:S(2)}) collective-permute-start(f32[200,128]{1,0:T(8,128)S(1)} %get-tuple-element.6), channel_id=1, source_target_pairs={{80,0},{96,16},{112,32},{128,48},{144,64},{160,80},{176,96},{192,1... | collective-permute-start | bytes 307208 | tf_op jit(solution)/shard_map/ppermute | solution.py:22
  276.5 4.7 %collective-permute-done.6 = f32[200,128]{1,0:T(8,128)S(1)} collective-permute-done((f32[200,128]{1,0:T(8,128)S(1)}, f32[200,128]{1,0:T(8,128)S(1)}, u32[]{:S(2)}, u32[]{:S(2)}) %collective-permute-start.6) | collective-permute-done | bytes 102432 | tf_op jit(solution)/shard_map/ppermute | solution.py:22
  281.2 0.0 collective-permute-done.7
  281.2 0.0 collective-permute-done.8
  281.3 0.0 collective-permute-done.9
  281.3 0.0 collective-permute-done.10
  281.3 0.0 copy-start.2
  281.4 0.7 stack.68
  282.2 0.1 copy-done.2
  (19 shorter events, 0.2 us)
Async XLA Ops:
  7.2 50.6 %all-gather.3.cloned.1.call-start = ((), (), s32[]{:S(2)}) async-start(), calls=%async_computation | async-start | bytes 1671168 | tf_op jit(solution)/shard_map/all_gather | solution.py:248
  7.2 8.4 %collective-permute-start = (f32[192,128]{1,0:T(8,128)}, f32[192,128]{1,0:T(8,128)S(1)}, u32[]{:S(2)}, u32[]{:S(2)}) collective-permute-start(f32[192,128]{1,0:T(8,128)} %bitcast.88), channel_id=1, source_target_pairs={{144,0},{160,16},{176,32},{192,48},{208,64},{224,80},{240,96},{0,1... | collective-permute-start | bytes 294920 | tf_op jit(solution)/shard_map/ppermute | solution.py:22
  15.6 0.6 copy-start.1
  16.3 137.6 %all-gather.5.cloned.1.call-start = ((), (), s32[]{:S(2)}) async-start(), calls=%async_computation.1 | async-start | bytes 17825792 | tf_op jit(solution)/shard_map/all_gather | solution.py:249
  17.8 6.5 %collective-permute-start.1 = (f32[1,2048]{1,0:T(1,128)S(1)}, f32[1,2048]{1,0:T(1,128)S(1)}, u32[]{:S(2)}, u32[]{:S(2)}) collective-permute-start(f32[1,2048]{1,0:T(1,128)S(1)} %multiply_exponential_fusion), channel_id=1, source_target_pairs={{240,0},{0,16},{16,32},{32,48},{48,64},{64,80},{80,96},{96,112},{1... | collective-permute-start | bytes 24584 | tf_op jit(solution)/shard_map/ppermute | solution.py:22
  24.3 7.2 %collective-permute-start.2 = (f32[2,2048]{1,0:T(2,128)S(1)}, f32[2,2048]{1,0:T(2,128)S(1)}, u32[]{:S(2)}, u32[]{:S(2)}) collective-permute-start(f32[2,2048]{1,0:T(2,128)S(1)} %pad_maximum_fusion.2), channel_id=1, source_target_pairs={{224,0},{240,16},{0,32},{16,48},{32,64},{48,80},{64,96},{80,112},{... | collective-permute-start | bytes 49160 | tf_op jit(solution)/shard_map/ppermute | solution.py:22
  31.5 9.3 %collective-permute-start.3 = (f32[4,2048]{1,0:T(4,128)S(1)}, f32[4,2048]{1,0:T(4,128)S(1)}, u32[]{:S(2)}, u32[]{:S(2)}) collective-permute-start(f32[4,2048]{1,0:T(4,128)S(1)} %pad_maximum_fusion.1), channel_id=1, source_target_pairs={{192,0},{208,16},{224,32},{240,48},{0,64},{16,80},{32,96},{48,112}... | collective-permute-start | bytes 98312 | tf_op jit(solution)/shard_map/ppermute | solution.py:22
  154.0 1.4 copy-start
  247.0 14.8 %collective-permute-start.4 = (f32[200,128]{1,0:T(8,128)S(1)}, f32[200,128]{1,0:T(8,128)S(1)}, u32[]{:S(2)}, u32[]{:S(2)}) collective-permute-start(f32[200,128]{1,0:T(8,128)S(1)} %get-tuple-element.8), channel_id=1, source_target_pairs={{112,0},{128,16},{144,32},{160,48},{176,64},{192,80},{208,96},{224... | collective-permute-start | bytes 307208 | tf_op jit(solution)/shard_map/ppermute | solution.py:22
  250.8 30.5 %collective-permute-start.10 = (f32[200,128]{1,0:T(8,128)S(1)}, f32[200,128]{1,0:T(8,128)S(1)}, u32[]{:S(2)}, u32[]{:S(2)}) collective-permute-start(f32[200,128]{1,0:T(8,128)S(1)} %get-tuple-element.2), channel_id=1, source_target_pairs={{16,0},{32,16},{48,32},{64,48},{80,64},{96,80},{112,96},{128,112},... | collective-permute-start | bytes 307208 | tf_op jit(solution)/shard_map/ppermute | solution.py:22
  252.7 28.6 %collective-permute-start.9 = (f32[200,128]{1,0:T(8,128)S(1)}, f32[200,128]{1,0:T(8,128)S(1)}, u32[]{:S(2)}, u32[]{:S(2)}) collective-permute-start(f32[200,128]{1,0:T(8,128)S(1)} %get-tuple-element.3), channel_id=1, source_target_pairs={{32,0},{48,16},{64,32},{80,48},{96,64},{112,80},{128,96},{144,112}... | collective-permute-start | bytes 307208 | tf_op jit(solution)/shard_map/ppermute | solution.py:22
  254.9 26.4 %collective-permute-start.8 = (f32[200,128]{1,0:T(8,128)S(1)}, f32[200,128]{1,0:T(8,128)S(1)}, u32[]{:S(2)}, u32[]{:S(2)}) collective-permute-start(f32[200,128]{1,0:T(8,128)S(1)} %get-tuple-element.4), channel_id=1, source_target_pairs={{48,0},{64,16},{80,32},{96,48},{112,64},{128,80},{144,96},{160,112... | collective-permute-start | bytes 307208 | tf_op jit(solution)/shard_map/ppermute | solution.py:22
  257.7 23.5 %collective-permute-start.7 = (f32[200,128]{1,0:T(8,128)S(1)}, f32[200,128]{1,0:T(8,128)S(1)}, u32[]{:S(2)}, u32[]{:S(2)}) collective-permute-start(f32[200,128]{1,0:T(8,128)S(1)} %get-tuple-element.5), channel_id=1, source_target_pairs={{64,0},{80,16},{96,32},{112,48},{128,64},{144,80},{160,96},{176,11... | collective-permute-start | bytes 307208 | tf_op jit(solution)/shard_map/ppermute | solution.py:22
  261.8 8.2 %collective-permute-start.5 = (f32[200,128]{1,0:T(8,128)S(1)}, f32[200,128]{1,0:T(8,128)S(1)}, u32[]{:S(2)}, u32[]{:S(2)}) collective-permute-start(f32[200,128]{1,0:T(8,128)S(1)} %get-tuple-element.7), channel_id=1, source_target_pairs={{96,0},{112,16},{128,32},{144,48},{160,64},{176,80},{192,96},{208,... | collective-permute-start | bytes 307208 | tf_op jit(solution)/shard_map/ppermute | solution.py:22
  270.1 11.2 %collective-permute-start.6 = (f32[200,128]{1,0:T(8,128)S(1)}, f32[200,128]{1,0:T(8,128)S(1)}, u32[]{:S(2)}, u32[]{:S(2)}) collective-permute-start(f32[200,128]{1,0:T(8,128)S(1)} %get-tuple-element.6), channel_id=1, source_target_pairs={{80,0},{96,16},{112,32},{128,48},{144,64},{160,80},{176,96},{192,1... | collective-permute-start | bytes 307208 | tf_op jit(solution)/shard_map/ppermute | solution.py:22
  281.3 0.9 copy-start.2
Sparse Core Ops, SparseCore 0:
  16.4 41.2 all-gather.2
  59.6 94.3 all-gather.4
